TPU v7x, 512 devices: a whole 4x4x16 slice. The times are simulated.
512 devices in a mesh: lat: 32 (over z, core), ch: 16 (over y, x).
Axes of the slice: x: 4, y: 4, z: 16, core: 2. Of those that a mesh axis runs over, the one named last changes fastest.
Arguments:
- fields: bfloat16 [2, 704, 32, 1440], P(None, 'lat', 'ch'), may hold values from -6 to 6
- table: bfloat16 [704, 704, 352], P('lat', 'ch'), may hold values from -1 to 1, as said below
Outputs:
- coefficients: float32 [704, 704, 128], P('lat', 'ch')
Inputs may be any that keep to these rules, and one draw needn't show every extreme that they name: table[m, l, k] is zero wherever l < m.
All inputs are finite; a program needn't handle non-finite values.
Results may differ from a plain program's by a relative error of at most 0.005.
Values may be sent and summed in bfloat16 or wider, within the bound.
A program may use at most 64 MiB of HBM per device.

v0:
```python
import math
import jax
import jax.numpy as jnp
from jax import lax
from jax.sharding import PartitionSpec as P

MODES = 704


def fourier_table(nlon, modes):
    cols = jnp.arange(nlon, dtype=jnp.int32)[:, None]
    orders = jnp.arange(modes, dtype=jnp.int32)[None, :]
    phase = (cols * orders % nlon).astype(jnp.float32) * (2.0 * math.pi / nlon)
    factor = 1.0 / math.sqrt(nlon)
    return jnp.concatenate([jnp.cos(phase) * factor, -jnp.sin(phase) * factor], axis=1).astype(
        jnp.bfloat16
    )


def parity_project(block, parts, order_start, degree_start):
    order_count, degree_count, hemisphere = block.shape
    padding = degree_count % 2
    first_rows = block[:, 0::2]
    second_rows = block[:, 1::2]
    orders = order_start + jnp.arange(order_count, dtype=jnp.int32)[:, None, None]
    aligned = (degree_start - orders) % 2 == 0
    sym_table = jnp.where(aligned, first_rows, second_rows)
    anti_table = jnp.where(aligned, second_rows, first_rows)
    sym_coeffs = jnp.einsum(
        "mlk,bkcrm->mlbcr", sym_table, parts[:, :hemisphere], preferred_element_type=jnp.float32
    )
    anti_coeffs = jnp.einsum(
        "mlk,bkcrm->mlbcr", anti_table, parts[:, hemisphere:], preferred_element_type=jnp.float32
    )
    chosen = aligned[:, :, :, None, None]
    first_out = jnp.where(chosen, sym_coeffs, anti_coeffs)
    second_out = jnp.where(chosen, anti_coeffs, sym_coeffs)
    joined = jnp.stack([first_out, second_out], axis=2)
    joined = joined.reshape((order_count, degree_count + padding) + sym_coeffs.shape[2:])
    return joined


def shards(fields, table):
    batch, rows, chans, nlon = fields.shape
    slab, lblock, half = table.shape
    fourier = fourier_table(nlon, MODES)
    spectrum = jnp.einsum("brcj,jn->brcn", fields, fourier, preferred_element_type=jnp.float32)
    spectrum = spectrum.astype(jnp.bfloat16).reshape(batch, rows, chans, 2, MODES)
    moved = lax.all_to_all(spectrum, "lat", split_axis=4, concat_axis=1, tiled=True)
    north = moved[:, :half].astype(jnp.float32)
    south = moved[:, half:][:, ::-1].astype(jnp.float32)
    parts = jnp.concatenate(
        [(north + south).astype(jnp.bfloat16), (north - south).astype(jnp.bfloat16)], axis=1
    )
    order_start = lax.axis_index("lat") * slab
    degree_start = lax.axis_index("ch") * lblock
    gathered = parity_project(
        table, lax.all_gather(parts, "ch", axis=2, tiled=True), order_start, degree_start
    )
    return gathered.reshape(slab, lblock, -1)


def solution(mesh):
    return jax.shard_map(
        shards,
        mesh=mesh,
        in_specs=(P(None, "lat", "ch", None), P("lat", "ch", None)),
        out_specs=P("lat", "ch", None),
        check_vma=False,
    )
```

profile of v0, /device:TPU:1, one launch (start us, length us, event | category | flops | bytes accessed | tf_op | source)
XLA Modules:
  0.0 162.0 jit_solution(14036317072984009875)
XLA Ops:
  6.5 19.1 %multiply_convert_fusion = (bf16[1440,704]{1,0:T(8,128)(2,1)S(1)}, bf16[1440,704]{1,0:T(8,128)(2,1)S(1)}) fusion(), kind=kLoop, calls=%fused_computation.3 | loop fusion | flops 14192640 | bytes 4055040 | tf_op jit(solution)/shard_map/convert.1
  25.7 1.0 fusion.7
  26.7 0.3 reshape.50
  27.0 1.8 %copy.24 = bf16[2,22,2,2,704]{1,3,2,0,4:T(2,128)(2,1)S(1)} copy(bf16[2,22,2,2,704]{4,3,1,2,0:T(2,128)(2,1)S(1)} %reshape.50) | data formatting | bytes 495616 | tf_op jit(solution)/shard_map/reshape | solution.py:48
  28.8 1.8 %reshape.51 = bf16[32,2,1936]{2,1,0:T(2,128)(2,1)S(1)} reshape(bf16[704,2,2,2,22]{4,3,2,1,0:T(2,128)(2,1)S(1)} %bitcast.45) | data formatting | bytes 495616
  30.6 38.8 %all_to_all.18 = bf16[32,2,1936]{2,1,0:T(2,128)(2,1)S(1)} all-to-all(bf16[32,2,1936]{2,1,0:T(2,128)(2,1)S(1)} %reshape.51), channel_id=1, replica_groups=mesh['lat'=32,'ch'=16] {'lat'}, dimensions={0} | all-to-all | bytes 495616 | tf_op jit(solution)/shard_map/all_to_all | solution.py:49
  69.5 1.8 %reshape.52 = bf16[704,2,2,2,22]{4,3,2,1,0:T(2,128)(2,1)S(1)} reshape(bf16[32,2,1936]{2,1,0:T(2,128)(2,1)S(1)} %all_to_all.18) | data formatting | bytes 495616
  71.3 0.4 copy.50
  71.7 2.9 %all_to_all.16 = bf16[2,704,2,2,22]{1,3,4,2,0:T(2,128)(2,1)S(1)} reshape(bf16[2,32,22,2,2,22]{2,1,4,5,3,0:T(8,128)(2,1)S(1)} %bitcast.44) | data formatting | bytes 495616 | tf_op jit(solution)/shard_map/all_to_all | solution.py:49
  74.6 0.2 slice.25
  74.9 0.8 reverse
  75.7 0.3 fusion.19
  76.0 0.1 fusion.20
  76.1 0.4 pad_maximum_fusion.1
  76.5 0.9 copy.27
  77.5 1.0 slice.18
  78.5 1.0 slice.19
  79.6 56.5 %all-gather.2.cloned.1.call-done = bf16[2,704,32,2,22]{1,3,4,0,2:T(2,128)(2,1)} async-done(((bf16[2,704,2,2,22]{1,3,4,0,2:T(2,128)(2,1)}), bf16[2,704,32,2,22]{1,3,4,0,2:T(2,128)(2,1)}) %all-gather.2.cloned.1.call-update) | async-done | bytes 3964944 | tf_op jit(solution)/shard_map/all_gather | solution.py:58
  136.1 6.5 %fusion.24 = (bf16[2,352,32,2,22]{1,3,4,0,2:T(2,128)(2,1)S(1)}, bf16[2,352,32,2,22]{1,3,4,0,2:T(2,128)(2,1)S(1)}) fusion(bf16[2,704,32,2,22]{1,3,4,0,2:T(2,128)(2,1)} %all-gather.2.cloned.1.call-done), kind=kLoop, calls=%fused_computation.39 | loop fusion | bytes 7929856 | tf_op jit(solution)/shard_map/slice | solution.py:30
  142.6 2.0 %fusion.8 = f32[22,22,2,32,2]{3,1,4,2,0:T(8,128)S(1)} fusion(bf16[2,352,32,2,22]{1,3,4,0,2:T(2,128)(2,1)S(1)} %get-tuple-element.8, bf16[22,22,352]{2,1,0:T(8,128)(2,1)S(1)} %slice.19, bf16[22,22,352]{2,1,0:T(8,128)(2,1)S(1)} %slice.18, pred[22]{0:T(512)(128)(4,1)S(1)} %fusion.21), kind=kOutput, calls=%fused_computation.14 | convolution fusion | flops 43784576 | bytes 2911766 | tf_op jit(solution)/shard_map/mlk,bkcrm->mlbcr/dot_general | solution.py:32
  144.6 2.0 %select_bitcast_fusion.1 = (f32[22,22,1,2,32,2]{4,1,5,3,0,2:T(8,128)S(1)}, f32[22,22,1,2,32,2]{4,1,5,3,0,2:T(8,128)S(1)}) fusion(f32[22,22,2,32,2]{3,1,4,2,0:T(8,128)S(1)} %fusion.8, pred[22]{0:T(512)(128)(4,1)S(1)} %fusion.21, bf16[2,352,32,2,22]{1,3,4,0,2:T(2,128)(2,1)S(1)} %get-tuple-element.7, bf16[22,22,352]{2,1,0:T(8,128)(2,1)S(1)} %slice.18, ...), kind=kOutput, calls=%fused_computation.20 | convolution fusion | flops 43908480 | bytes 3407382 | tf_op jit(solution)/shard_map/mlk,bkcrm->mlbcr/dot_general | solution.py:29
  146.6 1.6 pad_maximum_fusion
  148.2 5.0 %copy.30 = f32[22,22,2,2,32,2]{0,5,4,3,2,1:T(2,128)S(1)} copy(f32[22,22,2,2,32,2]{4,1,5,3,0,2:T(8,128)} %pad_maximum_fusion) | data formatting | bytes 991232 | tf_op jit(solution)/shard_map/stack | solution.py:38
  153.3 1.9 %copy.31 = f32[22,44,128]{2,1,0:T(8,128)} copy(f32[22,44,128]{0,2,1:T(8,128)S(1)} %bitcast.42) | data formatting | bytes 991232 | tf_op jit(solution)/shard_map/reshape;reshape | solution.py:60
  (9 shorter events, 0.1 us)
Async XLA Ops:
  6.5 19.1 %copy-start = (bf16[2,22,2,1440]{3,2,1,0:T(2,128)(2,1)S(1)}, bf16[2,22,2,1440]{3,2,1,0:T(2,128)(2,1)}, u32[]{:S(2)}) copy-start(bf16[2,22,2,1440]{3,2,1,0:T(2,128)(2,1)} %param.2) | copy-start | bytes 760324
  6.5 129.5 %all-gather.2.cloned.1.call-start = ((), (), s32[]{:S(2)}) async-start(), calls=%async_computation.1 | async-start | bytes 4595712 | tf_op jit(solution)/shard_map/all_gather | solution.py:58
  71.7 5.8 %copy-start.1 = (bf16[22,44,352]{2,1,0:T(8,128)(2,1)S(1)}, bf16[22,44,352]{2,1,0:T(8,128)(2,1)}, u32[]{:S(2)}) copy-start(bf16[22,44,352]{2,1,0:T(8,128)(2,1)} %param.3) | copy-start | bytes 2044420
  74.6 3.9 %copy-start.2 = (bf16[22,44,352]{2,1,0:T(8,128)(2,1)S(1)}, bf16[22,44,352]{2,1,0:T(8,128)(2,1)}, u32[]{:S(2)}) copy-start(bf16[22,44,352]{2,1,0:T(8,128)(2,1)} %param.3) | copy-start | bytes 2044420
Sparse Core Ops, SparseCore 0:
  77.6 58.4 all-gather.1
where the time goes:
time: 162 us
  waiting for transfers between devices  56.5 us (35%)
  blocking collectives  38.8 us (24%)
  local copies, waits for them, and re-layouts  26.6 us (16%)
  other arithmetic  21.5 us (13%)
  between operations  13.6 us (8%)
  matrix products  5.07 us (3%)
    all_gather x1, waiting for transfers between devices, shards(): lax.all_gather(parts, 'ch', axis=2, tiled=True)  56.5 us
    all_to_all x1, blocking collectives, shards(): lax.all_to_all(spectrum, 'lat', split_axis=4, concat_axis=1, tiled=True)  38.8 us
    another operation x1, other arithmetic  19.1 us
    slice x1, local copies, waits for them, and re-layouts, parity_project(): parts[:, :hemisphere]  6.52 us
    another operation x1, local copies, waits for them, and re-layouts, parity_project(): joined = jnp.stack([first_out, second_out], axis=2)  5.04 us
    unnamed x9, local copies, waits for them, and re-layouts  4.41 us
    all_to_all x2, local copies, waits for them, and re-layouts, shards(): lax.all_to_all(spectrum, 'lat', split_axis=4, concat_axis=1, tiled=True)  3.34 us
  transfers between devices with their start and end apart: 1, of which 1 were waited for; matrix products, arithmetic and copies ran while one was open for 1% of the time, Pallas kernels for 0%

commit v1 on v0

--- a/solution.py
+++ b/solution.py
@@ -55,7 +55,12 @@
     order_start = lax.axis_index("lat") * slab
     degree_start = lax.axis_index("ch") * lblock
     gathered = parity_project(
-        table, lax.all_gather(parts, "ch", axis=2, tiled=True), order_start, degree_start
+        table,
+        jnp.concatenate(
+            lax.all_to_all(jnp.stack([parts] * lax.axis_size("ch")), "ch", 0, 0), axis=2
+        ),
+        order_start,
+        degree_start,
     )
     return gathered.reshape(slab, lblock, -1)
 

time: 162 us -> 181 us (1.12)
  local copies, waits for them, and re-layouts: 26.6 us -> 42.5 us
  between operations: 13.6 us -> 0.15 us
  starting transfers between devices: 0.01 us -> 6.95 us
  waiting for transfers between devices: 56.5 us -> 62.2 us
  matrix products: 5.07 us -> 8.55 us
    all_to_all x0 -> x1, waiting for transfers between devices: none -> 62.2 us  [shards(): lax.all_to_all(jnp.stack([parts] * lax.axis_size('ch')), 'ch', 0, 0)]
    all_gather x1 -> x0, waiting for transfers between devices: 56.5 us -> none  [shards(): lax.all_gather(parts, 'ch', axis=2, tiled=True)]
    reshape x0 -> x2, local copies, waits for them, and re-layouts: none -> 18.9 us  [shards(): jnp.concatenate(lax.all_to_all(jnp.stack([parts] * lax.axis_size('ch')),...]
    all_to_all x0 -> x1, starting transfers between devices: none -> 6.95 us  [shards(): lax.all_to_all(jnp.stack([parts] * lax.axis_size('ch')), 'ch', 0, 0)]
    slice x1 -> x0, local copies, waits for them, and re-layouts: 6.52 us -> none  [parity_project(): parts[:, :hemisphere]]
    another operation x0 -> x1, local copies, waits for them, and re-layouts: none -> 4.27 us  [shards(): jnp.stack([parts] * lax.axis_size('ch'))]
    dot_general x1, matrix products: 2.01 us -> 3.86 us  [parity_project(): jnp.einsum('mlk,bkcrm->mlbcr', anti_table, parts[:, hemisphere:], preferr...]
    unnamed x9 -> x7, local copies, waits for them, and re-layouts: 4.41 us -> 4.4 us
where the time goes in v1:
time: 181 us
  waiting for transfers between devices  62.2 us (34%)
  local copies, waits for them, and re-layouts  42.5 us (23%)
  blocking collectives  38.8 us (21%)
  other arithmetic  21.5 us (12%)
  matrix products  8.55 us (5%)
  starting transfers between devices  6.95 us (4%)
    all_to_all x1, waiting for transfers between devices, shards(): lax.all_to_all(jnp.stack([parts] * lax.axis_size('ch')), 'ch', 0, 0)  62.2 us
    all_to_all x1, blocking collectives, shards(): lax.all_to_all(spectrum, 'lat', split_axis=4, concat_axis=1, tiled=True)  38.8 us
    another operation x1, other arithmetic  19.1 us
    reshape x2, local copies, waits for them, and re-layouts, shards(): jnp.concatenate(lax.all_to_all(jnp.stack([parts] * lax.axis_size('ch')),...  18.9 us
    all_to_all x1, starting transfers between devices, shards(): lax.all_to_all(jnp.stack([parts] * lax.axis_size('ch')), 'ch', 0, 0)  6.95 us
    another operation x1, local copies, waits for them, and re-layouts, parity_project(): joined = jnp.stack([first_out, second_out], axis=2)  5.04 us
    unnamed x7, local copies, waits for them, and re-layouts  4.4 us
    another operation x1, local copies, waits for them, and re-layouts, shards(): jnp.stack([parts] * lax.axis_size('ch'))  4.27 us
  transfers between devices with their start and end apart: 1, of which 1 were waited for; matrix products, arithmetic and copies ran while one was open for 1% of the time, Pallas kernels for 0%

profile of v1, /device:TPU:1, one launch (start us, length us, event | category | flops | bytes accessed | tf_op | source)
XLA Modules:
  0.0 180.7 jit_solution(7924179101784113105)
XLA Ops:
  0.0 19.1 %multiply_convert_fusion = (bf16[1440,704]{1,0:T(8,128)(2,1)S(1)}, bf16[1440,704]{1,0:T(8,128)(2,1)S(1)}) fusion(), kind=kLoop, calls=%fused_computation.3 | loop fusion | flops 14192640 | bytes 4055040 | tf_op jit(solution)/shard_map/convert.1
  19.1 1.0 fusion.7
  20.2 0.3 reshape.60
  20.5 1.8 %copy.21 = bf16[2,22,2,2,704]{1,3,2,0,4:T(2,128)(2,1)S(1)} copy(bf16[2,22,2,2,704]{4,3,1,2,0:T(2,128)(2,1)S(1)} %reshape.60) | data formatting | bytes 495616 | tf_op jit(solution)/shard_map/reshape | solution.py:48
  22.3 1.8 reshape.61
  24.1 38.8 %all_to_all.23 = bf16[32,2,1936]{2,1,0:T(2,128)(2,1)S(1)} all-to-all(bf16[32,2,1936]{2,1,0:T(2,128)(2,1)S(1)} %reshape.61), channel_id=1, replica_groups=mesh['lat'=32,'ch'=16] {'lat'}, dimensions={0} | all-to-all | bytes 495616 | tf_op jit(solution)/shard_map/all_to_all | solution.py:49
  62.9 1.8 reshape.62
  64.7 0.4 copy.38
  65.1 2.9 %all_to_all.19 = bf16[2,704,2,2,22]{1,3,4,2,0:T(2,128)(2,1)S(1)} reshape(bf16[2,32,22,2,2,22]{2,1,4,5,3,0:T(8,128)(2,1)S(1)} %bitcast.47) | data formatting | bytes 495616 | tf_op jit(solution)/shard_map/all_to_all | solution.py:49
  68.3 0.8 reverse
  69.1 0.3 fusion.19
  69.6 0.4 pad_maximum_fusion.1
  70.2 4.3 %stack.8 = bf16[16,2,704,2,2,22]{2,3,4,1,5,0:T(2,128)(2,1)} broadcast(bf16[2,704,2,2,22]{1,2,3,0,4:T(2,128)(2,1)S(1)} %copy.24), dimensions={1,2,3,4,5} | broadcast | bytes 4212736 | tf_op jit(solution)/shard_map/stack | solution.py:60
  74.5 6.9 %all-to-all-start.1 = ((bf16[16,2,704,2,2,22]{2,3,4,1,5,0:T(2,128)(2,1)}), bf16[16,2,704,2,2,22]{2,3,4,1,5,0:T(2,128)(2,1)}, u32[]{:S(2)}, u32[]{:S(2)}) async-start(bf16[16,2,704,2,2,22]{2,3,4,1,5,0:T(2,128)(2,1)} %stack.8), calls=%async_computation.1 | async-start | bytes 8650752 | tf_op jit(solution)/shard_map/all_to_all | solution.py:60
  81.4 1.0 slice.18
  82.5 1.0 slice.19
  83.6 62.2 %all-to-all-done.1 = bf16[16,2,704,2,2,22]{2,3,4,1,5,0:T(2,128)(2,1)} async-done(((bf16[16,2,704,2,2,22]{2,3,4,1,5,0:T(2,128)(2,1)}), bf16[16,2,704,2,2,22]{2,3,4,1,5,0:T(2,128)(2,1)}, u32[]{:S(2)}, u32[]{:S(2)}) %all-to-all-start.1) | async-done | bytes 3964960 | tf_op jit(solution)/shard_map/all_to_all | solution.py:60
  145.8 9.1 %copy.25 = bf16[2,704,16,2,2,22]{1,3,2,4,0,5:T(2,128)(2,1)} copy(bf16[2,704,16,2,2,22]{1,3,4,0,5,2:T(2,128)(2,1)} %bitcast.8) | data formatting | bytes 7929856 | tf_op jit(solution)/shard_map/reshape | solution.py:59
  154.9 9.8 %reshape.56 = bf16[2,704,32,2,22]{1,2,3,0,4:T(8,128)(2,1)} reshape(bf16[2,704,16,2,2,22]{1,3,2,4,0,5:T(2,128)(2,1)} %copy.25) | data formatting | bytes 7929856 | tf_op jit(solution)/shard_map/reshape | solution.py:59
  164.6 3.9 %fusion.8 = f32[22,22,2,32,2]{3,1,4,2,0:T(8,128)S(1)} fusion(bf16[2,704,32,2,22]{1,2,3,0,4:T(8,128)(2,1)} %reshape.56, bf16[22,22,352]{2,1,0:T(8,128)(2,1)S(1)} %slice.19, bf16[22,22,352]{2,1,0:T(8,128)(2,1)S(1)} %slice.18, pred[22]{0:T(512)(128)(4,1)S(1)} %fusion.21), kind=kOutput, calls=%fused_computation.13 | convolution fusion | flops 43784576 | bytes 3091990 | tf_op jit(solution)/shard_map/mlk,bkcrm->mlbcr/dot_general | solution.py:32
  168.5 3.6 %select_bitcast_fusion.1 = (f32[22,22,1,2,32,2]{4,1,5,3,0,2:T(8,128)S(1)}, f32[22,22,1,2,32,2]{4,1,5,3,0,2:T(8,128)S(1)}) fusion(f32[22,22,2,32,2]{3,1,4,2,0:T(8,128)S(1)} %fusion.8, pred[22]{0:T(512)(128)(4,1)S(1)} %fusion.21, bf16[2,704,32,2,22]{1,2,3,0,4:T(8,128)(2,1)} %reshape.56, bf16[22,22,352]{2,1,0:T(8,128)(2,1)S(1)} %slice.18, ...), kind=kOutput, calls=%fused_computation.20 | convolution fusion | flops 43908480 | bytes 4551680 | tf_op jit(solution)/shard_map/mlk,bkcrm->mlbcr/dot_general | solution.py:29
  172.1 1.6 pad_maximum_fusion
  173.7 5.0 %copy.26 = f32[22,22,2,2,32,2]{0,5,4,3,2,1:T(2,128)S(1)} copy(f32[22,22,2,2,32,2]{4,1,5,3,0,2:T(8,128)} %pad_maximum_fusion) | data formatting | bytes 991232 | tf_op jit(solution)/shard_map/stack | solution.py:38
  178.8 1.9 %copy.27 = f32[22,44,128]{2,1,0:T(8,128)} copy(f32[22,44,128]{0,2,1:T(8,128)S(1)} %bitcast.45) | data formatting | bytes 991232 | tf_op jit(solution)/shard_map/reshape;reshape | solution.py:65
  (8 shorter events, 0.6 us)
Async XLA Ops:
  0.0 19.1 %copy-start = (bf16[2,22,2,1440]{3,2,1,0:T(2,128)(2,1)S(1)}, bf16[2,22,2,1440]{3,2,1,0:T(2,128)(2,1)}, u32[]{:S(2)}) copy-start(bf16[2,22,2,1440]{3,2,1,0:T(2,128)(2,1)} %param.2) | copy-start | bytes 760324
  74.5 7.0 %copy-start.1 = (bf16[22,44,352]{2,1,0:T(8,128)(2,1)S(1)}, bf16[22,44,352]{2,1,0:T(8,128)(2,1)}, u32[]{:S(2)}) copy-start(bf16[22,44,352]{2,1,0:T(8,128)(2,1)} %param.3) | copy-start | bytes 2044420
  74.5 71.3 %all-to-all-start.1 = ((bf16[16,2,704,2,2,22]{2,3,4,1,5,0:T(2,128)(2,1)}), bf16[16,2,704,2,2,22]{2,3,4,1,5,0:T(2,128)(2,1)}, u32[]{:S(2)}, u32[]{:S(2)}) async-start(bf16[16,2,704,2,2,22]{2,3,4,1,5,0:T(2,128)(2,1)} %stack.8), calls=%async_computation.1 | async-start | bytes 8650752 | tf_op jit(solution)/shard_map/all_to_all | solution.py:60
